TPU v7x, 128 devices: a whole 4x4x4 slice. The times are simulated.
128 devices in a mesh: nodes: 16 (over x, z), cols: 8 (over y, core).
Axes of the slice: x: 4, y: 4, z: 4, core: 2. Of those that a mesh axis runs over, the one named last changes fastest.
Arguments:
- node_feats: bfloat16 [32768, 256], P(('nodes', 'cols')), may hold values from -6 to 6
- tile_row: int32 [16, 2816], P('nodes', 'cols'), may hold values from 0 to 15, as said below
- tile_col: int32 [16, 2816], P('nodes', 'cols'), may hold values from 0 to 31
- tile_bits: int32 [16, 2816, 16, 128], P('nodes', 'cols'), may hold values from 0 to 255, as said below
- w_self: bfloat16 [256, 256], replicated, may hold values from -0.375 to 0.375
- w_neigh: bfloat16 [256, 256], replicated, may hold values from -1.5 to 1.5
- bias: float32 [256], replicated, may hold values from -3 to 3
- cotangent: bfloat16 [32768, 256], P(('nodes', 'cols')), may hold values from -6 to 6
Outputs:
- layer_out: bfloat16 [32768, 256], P(('nodes', 'cols'))
- feat_grad: bfloat16 [32768, 256], P(('nodes', 'cols'))
- self_grad: float32 [256, 256], replicated
- neigh_grad: float32 [256, 256], replicated
- bias_grad: float32 [256], replicated
Inputs may be any that keep to these rules, and one draw needn't show every extreme that they name: `tile_row`: destination row block of a tile within its nodes group; in every nodes group at least one block carries no tile. `tile_col`: source row block of a tile within its cols index; a block may carry several tiles. `tile_bits`: bit j of word (w, a) of a tile is its edge from destination row a to source column 8 w + j; bits above the eighth are zero; some destination rows have no edge in any tile.
All inputs are finite; a program needn't handle non-finite values.
Results may differ from a plain program's by a relative error of at most 0.0075.
Values may be sent and summed in bfloat16 or wider, within the bound.
No kernel may reach another device: no remote copies, remote signals or barrier semaphores. Data moves between devices by JAX's collectives and lax.ppermute only.
A program may use at most 64 MiB of HBM per device.

v0:
```python
import math
import jax
import jax.numpy as jnp
from jax import lax
from jax.sharding import PartitionSpec as P


def unpack_tiles(packed):
    shifts = jnp.arange(8, dtype=jnp.int32)
    edge_flags = jnp.right_shift(packed[:, :, None, :], shifts[None, None, :, None]) & 1
    return edge_flags.reshape(packed.shape[0], 128, 128)


def shards(node_feats, tile_row, tile_col, tile_bits, w_self, w_neigh, bias, cotangent):
    rows_dev = node_feats.shape[0]
    width_in = node_feats.shape[1]
    node_count = lax.axis_size("nodes")
    col_count = lax.axis_size("cols")
    per_dev = rows_dev // 128
    dest_count = col_count * per_dev
    source_count = node_count * per_dev
    tile_count = tile_row.shape[1]
    tile_group = math.gcd(tile_count, 32)
    group_count = tile_count // tile_group
    rows_here = tile_row[0].reshape(group_count, tile_group)
    cols_here = tile_col[0].reshape(group_count, tile_group)
    packed_here = tile_bits[0].reshape(group_count, tile_group, 16, 128)
    source = lax.all_gather(node_feats, "nodes", axis=0, tiled=True)
    source_blocks = source.reshape(source_count, 128, width_in)

    def forward_step(totals, tile_set):
        summed, degree = totals
        rows_blk, cols_blk, packed_blk = tile_set
        edge_flags = unpack_tiles(packed_blk)
        bits_blk = edge_flags.astype(jnp.bfloat16)
        picked = source_blocks[cols_blk]
        products = jnp.einsum("tba,tbf->taf", bits_blk, picked, preferred_element_type=jnp.float32)
        summed = summed.at[rows_blk].add(products)
        degree = degree.at[rows_blk].add(jnp.sum(edge_flags, axis=1).astype(jnp.float32))
        return ((summed, degree), None)

    initial = (
        jnp.zeros((dest_count, 128, width_in), jnp.float32),
        jnp.zeros((dest_count, 128), jnp.float32),
    )
    (partial_sum, degree_part), _ = lax.scan(
        forward_step, initial, (rows_here, cols_here, packed_here)
    )
    summed, degree = (
        lax.psum_scatter(
            partial_sum.reshape(dest_count * 128, width_in), "cols", scatter_dimension=0, tiled=True
        ),
        lax.psum_scatter(
            degree_part.reshape(dest_count * 128), "cols", scatter_dimension=0, tiled=True
        ),
    )
    degree = jnp.maximum(degree, 1.0)
    neigh_mean = (summed / degree[:, None]).astype(jnp.bfloat16)
    preact = (
        jnp.dot(node_feats, w_self, preferred_element_type=jnp.float32)
        + jnp.dot(neigh_mean, w_neigh, preferred_element_type=jnp.float32)
        + bias
    )
    sigmoid_pre = jax.nn.sigmoid(preact)
    layer_out = (preact * sigmoid_pre).astype(jnp.bfloat16)
    pre_grad = (
        cotangent.astype(jnp.float32) * sigmoid_pre * (1.0 + preact * (1.0 - sigmoid_pre))
    ).astype(jnp.bfloat16)
    self_term = jnp.dot(node_feats.T, pre_grad, preferred_element_type=jnp.float32)
    neigh_term = jnp.dot(neigh_mean.T, pre_grad, preferred_element_type=jnp.float32)
    bias_term = jnp.sum(pre_grad.astype(jnp.float32), axis=0)
    self_grad, neigh_grad, bias_grad = lax.psum(
        (self_term, neigh_term, bias_term), ("nodes", "cols")
    )
    mean_grad = (
        jnp.dot(pre_grad, w_neigh.T, preferred_element_type=jnp.float32) / degree[:, None]
    ).astype(jnp.bfloat16)
    dest_grad = lax.all_gather(mean_grad, "cols", axis=0, tiled=True)
    grad_blocks = dest_grad.reshape(dest_count, 128, width_in)

    def backward_step(src_grad, tile_set):
        rows_blk, cols_blk, packed_blk = tile_set
        bits_blk = unpack_tiles(packed_blk).astype(jnp.bfloat16)
        picked = grad_blocks[rows_blk]
        products = jnp.einsum("tba,taf->tbf", bits_blk, picked, preferred_element_type=jnp.float32)
        return (src_grad.at[cols_blk].add(products), None)

    src_total, _ = lax.scan(
        backward_step,
        jnp.zeros((source_count, 128, width_in), jnp.float32),
        (rows_here, cols_here, packed_here),
    )
    src_total = src_total.reshape(source_count * 128, width_in)
    src_grad = lax.psum_scatter(src_total, "nodes", scatter_dimension=0, tiled=True)
    feat_grad = (jnp.dot(pre_grad, w_self.T, preferred_element_type=jnp.float32) + src_grad).astype(
        jnp.bfloat16
    )
    return (layer_out, feat_grad, self_grad, neigh_grad, bias_grad)


def solution(mesh):
    return jax.shard_map(
        shards,
        mesh=mesh,
        in_specs=(
            P(("nodes", "cols"), None),
            P("nodes", "cols"),
            P("nodes", "cols"),
            P("nodes", "cols", None, None),
            P(),
            P(),
            P(),
            P(("nodes", "cols"), None),
        ),
        out_specs=(P(("nodes", "cols"), None), P(("nodes", "cols"), None), P(), P(), P()),
        check_vma=False,
    )
```

profile of v0, /device:TPU:0, one launch (start us, length us, event | category | flops | bytes accessed | tf_op | source)
XLA Modules:
  0.0 557.2 jit_solution(13627646105467495376)
XLA Ops:
  9.5 48.4 %all-gather.3.cloned.1.call-done = bf16[4096,256]{1,0:T(8,128)(2,1)} async-done(((bf16[256,256]{1,0:T(8,128)(2,1)}), bf16[4096,256]{1,0:T(8,128)(2,1)}) %all-gather.3.cloned.1.call-update) | async-done | bytes 2097168 | tf_op jit(solution)/shard_map/all_gather | solution.py:28
  58.1 182.1 %while.22 = (s32[]{:T(128)}, f32[16,128,256]{2,1,0:T(8,128)S(1)}, f32[16,128]{1,0:T(8,128)S(1)}, s32[11,32]{1,0:T(8,128)S(1)}, s32[11,32,16,128]{3,2,1,0:T(8,128...) while((s32[]{:T(128)}, f32[16,128,256]{2,1,0:T(8,128)S(1)}, ...), condition=%wide.region_4.5_spmd, body=%wide.region_0.4_spmd.sunk | while | flops 272635072 | bytes 24165348 | solution.py:46
  58.2 3.6 gather_fusion
  62.9 4.4 fusion.56
  67.2 6.5 %scatter_fusion = f32[16,128,256]{2,1,0:T(8,128)S(1)} fusion(f32[16,128,256]{2,1,0:T(8,128)S(1)} %get-tuple-element.232, s32[32]{0:T(128)S(1)} %get-tuple-element.213, f32[32,128,256]{2,1,0:T(8,128)} %fusion.56), kind=kCustom, calls=%fused_computation.2.clone.1 | custom fusion | flops 1048576 | bytes 12583040 | tf_op jit(solution)/shard_map/while/body/eval_jaxpr/scatter-add | solution.py:38
  74.7 3.6 gather_fusion
  79.4 4.4 fusion.56
  83.8 6.5 %scatter_fusion = f32[16,128,256]{2,1,0:T(8,128)S(1)} fusion(f32[16,128,256]{2,1,0:T(8,128)S(1)} %get-tuple-element.232, s32[32]{0:T(128)S(1)} %get-tuple-element.213, f32[32,128,256]{2,1,0:T(8,128)} %fusion.56), kind=kCustom, calls=%fused_computation.2.clone.1 | custom fusion | flops 1048576 | bytes 12583040 | tf_op jit(solution)/shard_map/while/body/eval_jaxpr/scatter-add | solution.py:38
  91.3 3.6 gather_fusion
  96.0 4.4 fusion.56
  100.4 6.5 %scatter_fusion = f32[16,128,256]{2,1,0:T(8,128)S(1)} fusion(f32[16,128,256]{2,1,0:T(8,128)S(1)} %get-tuple-element.232, s32[32]{0:T(128)S(1)} %get-tuple-element.213, f32[32,128,256]{2,1,0:T(8,128)} %fusion.56), kind=kCustom, calls=%fused_computation.2.clone.1 | custom fusion | flops 1048576 | bytes 12583040 | tf_op jit(solution)/shard_map/while/body/eval_jaxpr/scatter-add | solution.py:38
  107.9 3.6 gather_fusion
  112.5 4.4 fusion.56
  116.9 6.5 %scatter_fusion = f32[16,128,256]{2,1,0:T(8,128)S(1)} fusion(f32[16,128,256]{2,1,0:T(8,128)S(1)} %get-tuple-element.232, s32[32]{0:T(128)S(1)} %get-tuple-element.213, f32[32,128,256]{2,1,0:T(8,128)} %fusion.56), kind=kCustom, calls=%fused_computation.2.clone.1 | custom fusion | flops 1048576 | bytes 12583040 | tf_op jit(solution)/shard_map/while/body/eval_jaxpr/scatter-add | solution.py:38
  124.4 3.6 gather_fusion
  129.1 4.4 fusion.56
  133.5 6.5 %scatter_fusion = f32[16,128,256]{2,1,0:T(8,128)S(1)} fusion(f32[16,128,256]{2,1,0:T(8,128)S(1)} %get-tuple-element.232, s32[32]{0:T(128)S(1)} %get-tuple-element.213, f32[32,128,256]{2,1,0:T(8,128)} %fusion.56), kind=kCustom, calls=%fused_computation.2.clone.1 | custom fusion | flops 1048576 | bytes 12583040 | tf_op jit(solution)/shard_map/while/body/eval_jaxpr/scatter-add | solution.py:38
  141.0 3.6 gather_fusion
  145.7 4.4 fusion.56
  150.0 6.5 %scatter_fusion = f32[16,128,256]{2,1,0:T(8,128)S(1)} fusion(f32[16,128,256]{2,1,0:T(8,128)S(1)} %get-tuple-element.232, s32[32]{0:T(128)S(1)} %get-tuple-element.213, f32[32,128,256]{2,1,0:T(8,128)} %fusion.56), kind=kCustom, calls=%fused_computation.2.clone.1 | custom fusion | flops 1048576 | bytes 12583040 | tf_op jit(solution)/shard_map/while/body/eval_jaxpr/scatter-add | solution.py:38
  157.5 3.6 gather_fusion
  162.2 4.4 fusion.56
  166.6 6.5 %scatter_fusion = f32[16,128,256]{2,1,0:T(8,128)S(1)} fusion(f32[16,128,256]{2,1,0:T(8,128)S(1)} %get-tuple-element.232, s32[32]{0:T(128)S(1)} %get-tuple-element.213, f32[32,128,256]{2,1,0:T(8,128)} %fusion.56), kind=kCustom, calls=%fused_computation.2.clone.1 | custom fusion | flops 1048576 | bytes 12583040 | tf_op jit(solution)/shard_map/while/body/eval_jaxpr/scatter-add | solution.py:38
  174.1 3.6 gather_fusion
  178.7 4.4 fusion.56
  183.1 6.5 %scatter_fusion = f32[16,128,256]{2,1,0:T(8,128)S(1)} fusion(f32[16,128,256]{2,1,0:T(8,128)S(1)} %get-tuple-element.232, s32[32]{0:T(128)S(1)} %get-tuple-element.213, f32[32,128,256]{2,1,0:T(8,128)} %fusion.56), kind=kCustom, calls=%fused_computation.2.clone.1 | custom fusion | flops 1048576 | bytes 12583040 | tf_op jit(solution)/shard_map/while/body/eval_jaxpr/scatter-add | solution.py:38
  190.6 3.6 gather_fusion
  195.3 4.4 fusion.56
  199.7 6.5 %scatter_fusion = f32[16,128,256]{2,1,0:T(8,128)S(1)} fusion(f32[16,128,256]{2,1,0:T(8,128)S(1)} %get-tuple-element.232, s32[32]{0:T(128)S(1)} %get-tuple-element.213, f32[32,128,256]{2,1,0:T(8,128)} %fusion.56), kind=kCustom, calls=%fused_computation.2.clone.1 | custom fusion | flops 1048576 | bytes 12583040 | tf_op jit(solution)/shard_map/while/body/eval_jaxpr/scatter-add | solution.py:38
  207.2 3.6 gather_fusion
  211.9 4.4 fusion.56
  216.2 6.5 %scatter_fusion = f32[16,128,256]{2,1,0:T(8,128)S(1)} fusion(f32[16,128,256]{2,1,0:T(8,128)S(1)} %get-tuple-element.232, s32[32]{0:T(128)S(1)} %get-tuple-element.213, f32[32,128,256]{2,1,0:T(8,128)} %fusion.56), kind=kCustom, calls=%fused_computation.2.clone.1 | custom fusion | flops 1048576 | bytes 12583040 | tf_op jit(solution)/shard_map/while/body/eval_jaxpr/scatter-add | solution.py:38
  223.7 3.6 gather_fusion
  228.4 4.4 fusion.56
  232.8 6.5 %scatter_fusion = f32[16,128,256]{2,1,0:T(8,128)S(1)} fusion(f32[16,128,256]{2,1,0:T(8,128)S(1)} %get-tuple-element.232, s32[32]{0:T(128)S(1)} %get-tuple-element.213, f32[32,128,256]{2,1,0:T(8,128)} %fusion.56), kind=kCustom, calls=%fused_computation.2.clone.1 | custom fusion | flops 1048576 | bytes 12583040 | tf_op jit(solution)/shard_map/while/body/eval_jaxpr/scatter-add | solution.py:38
  243.1 13.7 %all-reduce = f32[2048]{0:T(1024)S(1)} all-reduce(f32[2048]{0:T(1024)S(1)} %bitcast.96), channel_id=3, replica_groups=mesh['nodes'=16,'cols'=8] {'cols'}, use_global_device_ids=true, to_apply=%region_6.7.clone | all-reduce | flops 2048 | bytes 16384
  256.9 17.8 %reduce-scatter.3.cloned.1.call-done = f32[256,256]{1,0:T(8,128)} async-done(((f32[2048,256]{1,0:T(8,128)}), f32[256,256]{1,0:T(8,128)}) %reduce-scatter.3.cloned.1.call-update) | async-done | bytes 262160 | tf_op jit(solution)/shard_map/reduce_scatter | solution.py:50
  274.7 2.6 convert_reduce_fusion
  280.3 20.2 %all-gather.5.cloned.1.call-done = bf16[2048,256]{1,0:T(8,128)(2,1)} async-done(((bf16[256,256]{1,0:T(8,128)(2,1)}), bf16[2048,256]{1,0:T(8,128)(2,1)}) %all-gather.5.cloned.1.call-update) | async-done | bytes 1048592 | tf_op jit(solution)/shard_map/all_gather | solution.py:78
  302.9 166.3 %while.23 = (s32[]{:T(128)}, f32[32,128,256]{2,1,0:T(8,128)}, s32[11,32]{1,0:T(8,128)}, s32[11,32,16,128]{3,2,1,0:T(8,128)}, s32[11,32]{1,0:T(8,128)}, /*index=5*/bf16[16,128,256]{2,1,0:T(8,128)(2,1)S(1)}, s32[]{:T(128)}) while((s32[]{:T(128)}, f32[32,128,256]{2,1,0:T(8,128)}, s32[11,32]{1,0:T(8,128)}, s32[11,32,16,128]{3,2,1,0:T(8,128)}, ...), condition=%wide.region_9.10_spmd, body=%wide.region_7.9_spmd.sunk | while | flops 271058112 | bytes 23862236 | solution.py:88
  305.4 2.7 fusion.60
  308.1 9.9 %scatter_fusion.1 = f32[32,128,256]{2,1,0:T(8,128)} fusion(f32[32,128,256]{2,1,0:T(8,128)} %get-tuple-element.255, s32[32]{0:T(128)S(1)} %get-tuple-element.221, f32[32,128,256]{2,1,0:T(8,128)} %fusion.60), kind=kCustom, calls=%fused_computation.4.clone.1 | custom fusion | flops 1048576 | bytes 12583040 | tf_op jit(solution)/shard_map/while/body/eval_jaxpr/scatter-add | solution.py:86
  320.4 2.7 fusion.60
  323.2 9.9 %scatter_fusion.1 = f32[32,128,256]{2,1,0:T(8,128)} fusion(f32[32,128,256]{2,1,0:T(8,128)} %get-tuple-element.255, s32[32]{0:T(128)S(1)} %get-tuple-element.221, f32[32,128,256]{2,1,0:T(8,128)} %fusion.60), kind=kCustom, calls=%fused_computation.4.clone.1 | custom fusion | flops 1048576 | bytes 12583040 | tf_op jit(solution)/shard_map/while/body/eval_jaxpr/scatter-add | solution.py:86
  335.5 2.7 fusion.60
  338.3 9.9 %scatter_fusion.1 = f32[32,128,256]{2,1,0:T(8,128)} fusion(f32[32,128,256]{2,1,0:T(8,128)} %get-tuple-element.255, s32[32]{0:T(128)S(1)} %get-tuple-element.221, f32[32,128,256]{2,1,0:T(8,128)} %fusion.60), kind=kCustom, calls=%fused_computation.4.clone.1 | custom fusion | flops 1048576 | bytes 12583040 | tf_op jit(solution)/shard_map/while/body/eval_jaxpr/scatter-add | solution.py:86
  350.6 2.7 fusion.60
  353.3 9.9 %scatter_fusion.1 = f32[32,128,256]{2,1,0:T(8,128)} fusion(f32[32,128,256]{2,1,0:T(8,128)} %get-tuple-element.255, s32[32]{0:T(128)S(1)} %get-tuple-element.221, f32[32,128,256]{2,1,0:T(8,128)} %fusion.60), kind=kCustom, calls=%fused_computation.4.clone.1 | custom fusion | flops 1048576 | bytes 12583040 | tf_op jit(solution)/shard_map/while/body/eval_jaxpr/scatter-add | solution.py:86
  365.7 2.7 fusion.60
  368.4 9.9 %scatter_fusion.1 = f32[32,128,256]{2,1,0:T(8,128)} fusion(f32[32,128,256]{2,1,0:T(8,128)} %get-tuple-element.255, s32[32]{0:T(128)S(1)} %get-tuple-element.221, f32[32,128,256]{2,1,0:T(8,128)} %fusion.60), kind=kCustom, calls=%fused_computation.4.clone.1 | custom fusion | flops 1048576 | bytes 12583040 | tf_op jit(solution)/shard_map/while/body/eval_jaxpr/scatter-add | solution.py:86
  380.8 2.7 fusion.60
  383.5 10.0 %scatter_fusion.1 = f32[32,128,256]{2,1,0:T(8,128)} fusion(f32[32,128,256]{2,1,0:T(8,128)} %get-tuple-element.255, s32[32]{0:T(128)S(1)} %get-tuple-element.221, f32[32,128,256]{2,1,0:T(8,128)} %fusion.60), kind=kCustom, calls=%fused_computation.4.clone.1 | custom fusion | flops 1048576 | bytes 12583040 | tf_op jit(solution)/shard_map/while/body/eval_jaxpr/scatter-add | solution.py:86
  395.9 2.7 fusion.60
  398.7 10.2 %scatter_fusion.1 = f32[32,128,256]{2,1,0:T(8,128)} fusion(f32[32,128,256]{2,1,0:T(8,128)} %get-tuple-element.255, s32[32]{0:T(128)S(1)} %get-tuple-element.221, f32[32,128,256]{2,1,0:T(8,128)} %fusion.60), kind=kCustom, calls=%fused_computation.4.clone.1 | custom fusion | flops 1048576 | bytes 12583040 | tf_op jit(solution)/shard_map/while/body/eval_jaxpr/scatter-add | solution.py:86
  411.3 2.7 fusion.60
  414.1 9.9 %scatter_fusion.1 = f32[32,128,256]{2,1,0:T(8,128)} fusion(f32[32,128,256]{2,1,0:T(8,128)} %get-tuple-element.255, s32[32]{0:T(128)S(1)} %get-tuple-element.221, f32[32,128,256]{2,1,0:T(8,128)} %fusion.60), kind=kCustom, calls=%fused_computation.4.clone.1 | custom fusion | flops 1048576 | bytes 12583040 | tf_op jit(solution)/shard_map/while/body/eval_jaxpr/scatter-add | solution.py:86
  426.4 2.7 fusion.60
  429.1 10.0 %scatter_fusion.1 = f32[32,128,256]{2,1,0:T(8,128)} fusion(f32[32,128,256]{2,1,0:T(8,128)} %get-tuple-element.255, s32[32]{0:T(128)S(1)} %get-tuple-element.221, f32[32,128,256]{2,1,0:T(8,128)} %fusion.60), kind=kCustom, calls=%fused_computation.4.clone.1 | custom fusion | flops 1048576 | bytes 12583040 | tf_op jit(solution)/shard_map/while/body/eval_jaxpr/scatter-add | solution.py:86
  441.6 2.7 fusion.60
  444.3 9.9 %scatter_fusion.1 = f32[32,128,256]{2,1,0:T(8,128)} fusion(f32[32,128,256]{2,1,0:T(8,128)} %get-tuple-element.255, s32[32]{0:T(128)S(1)} %get-tuple-element.221, f32[32,128,256]{2,1,0:T(8,128)} %fusion.60), kind=kCustom, calls=%fused_computation.4.clone.1 | custom fusion | flops 1048576 | bytes 12583040 | tf_op jit(solution)/shard_map/while/body/eval_jaxpr/scatter-add | solution.py:86
  456.7 2.7 fusion.60
  459.4 9.8 %scatter_fusion.1 = f32[32,128,256]{2,1,0:T(8,128)} fusion(f32[32,128,256]{2,1,0:T(8,128)} %get-tuple-element.255, s32[32]{0:T(128)S(1)} %get-tuple-element.221, f32[32,128,256]{2,1,0:T(8,128)} %fusion.60), kind=kCustom, calls=%fused_computation.4.clone.1 | custom fusion | flops 1048576 | bytes 12583040 | tf_op jit(solution)/shard_map/while/body/eval_jaxpr/scatter-add | solution.py:86
  469.8 66.2 %psum.23 = f32[256]{0:T(256)} all-reduce(f32[256]{0:T(256)S(1)} %copy-done.7), channel_id=1, replica_groups=mesh['nodes'=16,'cols'=8] {'nodes','cols'}, use_global_device_ids=true, to_apply=%region_14.15 | all-reduce | flops 256 | bytes 2048 | tf_op jit(solution)/shard_map/psum | solution.py:72
  537.9 9.3 %reduce-scatter.5.cloned.1.call-done = f32[256,256]{1,0:T(8,128)} async-done(((f32[4096,256]{1,0:T(8,128)}), f32[256,256]{1,0:T(8,128)}) %reduce-scatter.5.cloned.1.call-update) | async-done | bytes 262160 | tf_op jit(solution)/shard_map/reduce_scatter | solution.py:94
  (194 shorter events, 65.4 us)
Async XLA Ops:
  7.2 267.5 %copy-start = (bf16[256,256]{1,0:T(8,128)(2,1)S(1)}, bf16[256,256]{1,0:T(8,128)(2,1)}, u32[]{:S(2)}) copy-start(bf16[256,256]{1,0:T(8,128)(2,1)} %param.17) | copy-start | bytes 393220
  7.2 50.7 %all-gather.3.cloned.1.call-start = ((), (), s32[]{:S(2)}) async-start(), calls=%async_computation.2 | async-start | bytes 2228224 | tf_op jit(solution)/shard_map/all_gather | solution.py:28
  7.9 266.8 %reduce-scatter.3.cloned.1.call-start = ((), (), s32[]{:S(2)}) async-start(), calls=%async_computation.3 | async-start | bytes 2359296 | tf_op jit(solution)/shard_map/reduce_scatter | solution.py:50
  240.2 1.4 copy-start.1
  240.2 2.0 copy-start.5
  240.2 2.0 copy-start.6
  240.3 1.4 copy-start.11
  240.3 2.6 copy-start.3
  240.3 2.6 copy-start.4
  240.3 34.4 %copy-start.9 = (bf16[256,256]{1,0:T(8,128)(2,1)S(1)}, bf16[256,256]{1,0:T(8,128)(2,1)}, u32[]{:S(2)}) copy-start(bf16[256,256]{1,0:T(8,128)(2,1)} %param.19) | copy-start | bytes 393220
  240.3 34.4 %copy-start.10 = (f32[256]{0:T(256)S(1)}, f32[256]{0:T(256)}, u32[]{:S(2)}) copy-start(f32[256]{0:T(256)} %param.18) | copy-start | bytes 3076
  241.6 58.9 %all-gather.5.cloned.1.call-start = ((), (), s32[]{:S(2)}) async-start(), calls=%async_computation.4 | async-start | bytes 1179648 | tf_op jit(solution)/shard_map/all_gather | solution.py:78
  274.7 4.5 copy-start.8
  278.2 257.9 %all-reduce.4.cloned.1.call-start = ((), (), s32[]{:S(2)}) async-start(), calls=%async_computation.6 | async-start | bytes 1048576 | tf_op jit(solution)/shard_map/psum | solution.py:72
  280.2 267.0 %reduce-scatter.5.cloned.1.call-start = ((), (), s32[]{:S(2)}) async-start(), calls=%async_computation.5 | async-start | bytes 4456448 | tf_op jit(solution)/shard_map/reduce_scatter | solution.py:94
  300.5 2.4 copy-start.2
  469.2 0.7 copy-start.7
Sparse Core Ops, SparseCore 0:
  10.2 47.7 all-gather.2
  241.7 32.9 reduce-scatter.2
  278.3 22.1 all-gather.4
  305.8 144.6 all-reduce.3
  469.3 77.8 reduce-scatter.4
where the time goes:
time: 560 us; the launch traced here: 557 us
  other arithmetic  200 us (36%)
  waiting for transfers between devices  96.4 us (17%)
  matrix products  85.6 us (15%)
  blocking collectives  80 us (14%)
  local copies, waits for them, and re-layouts  79.4 us (14%)
  between operations  14.6 us (3%)
    scatter-add x11, other arithmetic, backward_step(): return (src_grad.at[cols_blk].add(products), None)  109 us
    scatter-add x11, other arithmetic, forward_step(): summed = summed.at[rows_blk].add(products)  71.1 us
    psum x1, blocking collectives, shards(): lax.psum((self_term, neigh_term, bias_term), ('nodes', 'cols'))  66.2 us
    all_gather x1, waiting for transfers between devices, shards(): source = lax.all_gather(node_feats, 'nodes', axis=0, tiled=True)  48.4 us
    dot_general x11, matrix products, forward_step(): jnp.einsum('tba,tbf->taf', bits_blk, picked, preferred_element_type=jnp.f...  48.1 us
    gather x11, local copies, waits for them, and re-layouts, forward_step(): picked = source_blocks[cols_blk]  39.8 us
    dot_general x11, matrix products, backward_step(): jnp.einsum('tba,taf->tbf', bits_blk, picked, preferred_element_type=jnp.f...  30.1 us
    shift_right_arithmetic x66, local copies, waits for them, and re-layouts, unpack_tiles(): jnp.right_shift(packed[:, :, None, :], shifts[None, None, :, None]) & 1  23.4 us
  transfers between devices with their start and end apart: 5, of which 4 were waited for; matrix products, arithmetic and copies ran while one was open for 31% of the time, Pallas kernels for 0%

commit v1 on v0

--- a/solution.py
+++ b/solution.py
@@ -3,6 +3,28 @@
 import jax.numpy as jnp
 from jax import lax
 from jax.sharding import PartitionSpec as P
+
+
+def laid_out(parts, dim):
+    parts = jnp.moveaxis(parts, 0, dim)
+    shape = parts.shape
+    return parts.reshape(*shape[:dim], shape[dim] * shape[dim + 1], *shape[dim + 2 :])
+
+
+def ring_gather(value, axis, dim):
+    length = lax.axis_size(axis)
+    pairs = [(i, (i + 1) % length) for i in range(length)]
+    back = [(b, a) for a, b in pairs]
+    lower, upper = ([], [])
+    for step in range(length - 1):
+        if step % 2 == 0:
+            lower.append(lax.ppermute(lower[-1] if lower else value, axis, pairs))
+        else:
+            upper.append(lax.ppermute(upper[-1] if upper else value, axis, back))
+    pieces = jnp.stack([*lower[::-1], value, *upper])
+    shift = lax.axis_index(axis) - len(lower)
+    pieces = pieces[(jnp.arange(length) - shift) % length]
+    return laid_out(pieces, dim)
 
 
 def unpack_tiles(packed):
@@ -25,7 +47,7 @@
     rows_here = tile_row[0].reshape(group_count, tile_group)
     cols_here = tile_col[0].reshape(group_count, tile_group)
     packed_here = tile_bits[0].reshape(group_count, tile_group, 16, 128)
-    source = lax.all_gather(node_feats, "nodes", axis=0, tiled=True)
+    source = ring_gather(node_feats, "nodes", 0)
     source_blocks = source.reshape(source_count, 128, width_in)
 
     def forward_step(totals, tile_set):

time: 560 us -> 594 us (1.061)
  starting transfers between devices: 0.2 us -> 40.5 us
  waiting for transfers between devices: 96.4 us -> 75.2 us
  local copies, waits for them, and re-layouts: 79.4 us -> 88 us
  other arithmetic: 200 us -> 207 us
    all_gather x1 -> x0, waiting for transfers between devices: 48.4 us -> none  [shards(): source = lax.all_gather(node_feats, 'nodes', axis=0, tiled=True)]
    ppermute x0 -> x15, starting transfers between devices: none -> 40.2 us  [the longest x7 38.1 us: ring_gather(): upper.append(lax.ppermute(upper[-1] if upper else value, axis, back))]
    ppermute x0 -> x15, waiting for transfers between devices: none -> 26.2 us  [the longest x8 26.2 us: ring_gather(): lower.append(lax.ppermute(lower[-1] if lower else value, axis, pairs))]
    select_n x11, other arithmetic: 0.13 us -> 7.62 us  [forward_step(): summed = summed.at[rows_blk].add(products)]
  transfers between devices with their start and end apart: 5 -> 19, of which waited for: 4 -> 12; matrix products, arithmetic and copies ran while one was open for 31% -> 31% of each run, Pallas kernels for 0% -> 0%
where the time goes in v1:
time: 594 us; the launch traced here: 591 us
  other arithmetic  207 us (35%)
  local copies, waits for them, and re-layouts  88 us (15%)
  matrix products  85.9 us (14%)
  blocking collectives  78.4 us (13%)
  waiting for transfers between devices  75.2 us (13%)
  starting transfers between devices  40.5 us (7%)
  between operations  14.7 us (2%)
    scatter-add x11, other arithmetic, backward_step(): return (src_grad.at[cols_blk].add(products), None)  109 us
    scatter-add x11, other arithmetic, forward_step(): summed = summed.at[rows_blk].add(products)  71.1 us
    psum x1, blocking collectives, shards(): lax.psum((self_term, neigh_term, bias_term), ('nodes', 'cols'))  65.7 us
    dot_general x11, matrix products, forward_step(): jnp.einsum('tba,tbf->taf', bits_blk, picked, preferred_element_type=jnp.f...  48.4 us
    gather x11, local copies, waits for them, and re-layouts, forward_step(): picked = source_blocks[cols_blk]  39.8 us
    ppermute x7, starting transfers between devices, ring_gather(): upper.append(lax.ppermute(upper[-1] if upper else value, axis, back))  38.1 us
    dot_general x11, matrix products, backward_step(): jnp.einsum('tba,taf->tbf', bits_blk, picked, preferred_element_type=jnp.f...  30 us
    ppermute x8, waiting for transfers between devices, ring_gather(): lower.append(lax.ppermute(lower[-1] if lower else value, axis, pairs))  26.2 us
  transfers between devices with their start and end apart: 19, of which 12 were waited for; matrix products, arithmetic and copies ran while one was open for 31% of the time, Pallas kernels for 0%

profile of v1, /device:TPU:0, one launch (start us, length us, event | category | flops | bytes accessed | tf_op | source)
XLA Modules:
  0.0 590.8 jit_solution(16436282865309903777)
XLA Ops:
  9.3 8.0 %collective-permute-done = bf16[256,256]{1,0:T(8,128)(2,1)S(1)} collective-permute-done((bf16[256,256]{1,0:T(8,128)(2,1)}, bf16[256,256]{1,0:T(8,128)(2,1)S(1)}, u32[]{:S(2)}, u32[]{:S(2)}) %collective-permute-start) | collective-permute-done | bytes 131104 | tf_op jit(solution)/shard_map/ppermute | solution.py:21
  17.3 5.3 collective-permute-start.8
  22.7 2.9 collective-permute-done.1
  25.6 5.6 collective-permute-start.9
  31.2 2.7 collective-permute-done.2
  33.9 5.6 collective-permute-start.10
  39.5 2.7 collective-permute-done.3
  42.2 5.6 collective-permute-start.11
  51.1 4.9 collective-permute-start.12
  56.0 3.3 collective-permute-done.5
  59.4 5.8 collective-permute-start.13
  65.2 3.5 collective-permute-done.6
  71.5 5.4 collective-permute-start.14
  84.2 189.8 %while.22 = (s32[]{:T(128)}, f32[16,128,256]{2,1,0:T(8,128)S(1)}, f32[16,128]{1,0:T(8,128)S(1)}, s32[11,32]{1,0:T(8,128)}, s32[11,32,16,128]{3,2,1,0:T(8,128)}, ...) while((s32[]{:T(128)}, f32[16,128,256]{2,1,0:T(8,128)S(1)}, f32[16,128]{1,0:T(8,128)S(1)}, ...), condition=%wide.region_4.5_spmd, body=%wide.region_0.4_spmd.sunk | while | flops 272635072 | bytes 24165348 | solution.py:68
  84.9 3.6 gather_fusion
  89.5 4.4 fusion.58
  94.0 6.5 %scatter_fusion = f32[16,128,256]{2,1,0:T(8,128)S(1)} fusion(f32[16,128,256]{2,1,0:T(8,128)S(1)} %get-tuple-element.232, s32[32]{0:T(128)S(1)} %get-tuple-element.213, f32[32,128,256]{2,1,0:T(8,128)} %fusion.58), kind=kCustom, calls=%fused_computation.3.clone.1 | custom fusion | flops 1048576 | bytes 12583040 | tf_op jit(solution)/shard_map/while/body/eval_jaxpr/scatter-add | solution.py:60
  102.1 3.6 gather_fusion
  106.8 4.4 fusion.58
  111.2 6.5 %scatter_fusion = f32[16,128,256]{2,1,0:T(8,128)S(1)} fusion(f32[16,128,256]{2,1,0:T(8,128)S(1)} %get-tuple-element.232, s32[32]{0:T(128)S(1)} %get-tuple-element.213, f32[32,128,256]{2,1,0:T(8,128)} %fusion.58), kind=kCustom, calls=%fused_computation.3.clone.1 | custom fusion | flops 1048576 | bytes 12583040 | tf_op jit(solution)/shard_map/while/body/eval_jaxpr/scatter-add | solution.py:60
  119.4 3.6 gather_fusion
  124.1 4.4 fusion.58
  128.5 6.5 %scatter_fusion = f32[16,128,256]{2,1,0:T(8,128)S(1)} fusion(f32[16,128,256]{2,1,0:T(8,128)S(1)} %get-tuple-element.232, s32[32]{0:T(128)S(1)} %get-tuple-element.213, f32[32,128,256]{2,1,0:T(8,128)} %fusion.58), kind=kCustom, calls=%fused_computation.3.clone.1 | custom fusion | flops 1048576 | bytes 12583040 | tf_op jit(solution)/shard_map/while/body/eval_jaxpr/scatter-add | solution.py:60
  136.6 3.6 gather_fusion
  141.3 4.4 fusion.58
  145.7 6.5 %scatter_fusion = f32[16,128,256]{2,1,0:T(8,128)S(1)} fusion(f32[16,128,256]{2,1,0:T(8,128)S(1)} %get-tuple-element.232, s32[32]{0:T(128)S(1)} %get-tuple-element.213, f32[32,128,256]{2,1,0:T(8,128)} %fusion.58), kind=kCustom, calls=%fused_computation.3.clone.1 | custom fusion | flops 1048576 | bytes 12583040 | tf_op jit(solution)/shard_map/while/body/eval_jaxpr/scatter-add | solution.py:60
  153.9 3.6 gather_fusion
  158.6 4.4 fusion.58
  163.0 6.5 %scatter_fusion = f32[16,128,256]{2,1,0:T(8,128)S(1)} fusion(f32[16,128,256]{2,1,0:T(8,128)S(1)} %get-tuple-element.232, s32[32]{0:T(128)S(1)} %get-tuple-element.213, f32[32,128,256]{2,1,0:T(8,128)} %fusion.58), kind=kCustom, calls=%fused_computation.3.clone.1 | custom fusion | flops 1048576 | bytes 12583040 | tf_op jit(solution)/shard_map/while/body/eval_jaxpr/scatter-add | solution.py:60
  171.1 3.6 gather_fusion
  175.8 4.4 fusion.58
  180.2 6.5 %scatter_fusion = f32[16,128,256]{2,1,0:T(8,128)S(1)} fusion(f32[16,128,256]{2,1,0:T(8,128)S(1)} %get-tuple-element.232, s32[32]{0:T(128)S(1)} %get-tuple-element.213, f32[32,128,256]{2,1,0:T(8,128)} %fusion.58), kind=kCustom, calls=%fused_computation.3.clone.1 | custom fusion | flops 1048576 | bytes 12583040 | tf_op jit(solution)/shard_map/while/body/eval_jaxpr/scatter-add | solution.py:60
  188.4 3.6 gather_fusion
  193.1 4.4 fusion.58
  197.5 6.5 %scatter_fusion = f32[16,128,256]{2,1,0:T(8,128)S(1)} fusion(f32[16,128,256]{2,1,0:T(8,128)S(1)} %get-tuple-element.232, s32[32]{0:T(128)S(1)} %get-tuple-element.213, f32[32,128,256]{2,1,0:T(8,128)} %fusion.58), kind=kCustom, calls=%fused_computation.3.clone.1 | custom fusion | flops 1048576 | bytes 12583040 | tf_op jit(solution)/shard_map/while/body/eval_jaxpr/scatter-add | solution.py:60
  205.6 3.6 gather_fusion
  210.3 4.4 fusion.58
  214.7 6.5 %scatter_fusion = f32[16,128,256]{2,1,0:T(8,128)S(1)} fusion(f32[16,128,256]{2,1,0:T(8,128)S(1)} %get-tuple-element.232, s32[32]{0:T(128)S(1)} %get-tuple-element.213, f32[32,128,256]{2,1,0:T(8,128)} %fusion.58), kind=kCustom, calls=%fused_computation.3.clone.1 | custom fusion | flops 1048576 | bytes 12583040 | tf_op jit(solution)/shard_map/while/body/eval_jaxpr/scatter-add | solution.py:60
  222.9 3.6 gather_fusion
  227.6 4.4 fusion.58
  232.0 6.5 %scatter_fusion = f32[16,128,256]{2,1,0:T(8,128)S(1)} fusion(f32[16,128,256]{2,1,0:T(8,128)S(1)} %get-tuple-element.232, s32[32]{0:T(128)S(1)} %get-tuple-element.213, f32[32,128,256]{2,1,0:T(8,128)} %fusion.58), kind=kCustom, calls=%fused_computation.3.clone.1 | custom fusion | flops 1048576 | bytes 12583040 | tf_op jit(solution)/shard_map/while/body/eval_jaxpr/scatter-add | solution.py:60
  240.1 3.6 gather_fusion
  244.8 4.4 fusion.58
  249.2 6.5 %scatter_fusion = f32[16,128,256]{2,1,0:T(8,128)S(1)} fusion(f32[16,128,256]{2,1,0:T(8,128)S(1)} %get-tuple-element.232, s32[32]{0:T(128)S(1)} %get-tuple-element.213, f32[32,128,256]{2,1,0:T(8,128)} %fusion.58), kind=kCustom, calls=%fused_computation.3.clone.1 | custom fusion | flops 1048576 | bytes 12583040 | tf_op jit(solution)/shard_map/while/body/eval_jaxpr/scatter-add | solution.py:60
  257.4 3.6 gather_fusion
  262.1 4.4 fusion.58
  266.5 6.5 %scatter_fusion = f32[16,128,256]{2,1,0:T(8,128)S(1)} fusion(f32[16,128,256]{2,1,0:T(8,128)S(1)} %get-tuple-element.232, s32[32]{0:T(128)S(1)} %get-tuple-element.213, f32[32,128,256]{2,1,0:T(8,128)} %fusion.58), kind=kCustom, calls=%fused_computation.3.clone.1 | custom fusion | flops 1048576 | bytes 12583040 | tf_op jit(solution)/shard_map/while/body/eval_jaxpr/scatter-add | solution.py:60
  276.8 12.7 %all-reduce = f32[2048]{0:T(1024)S(1)} all-reduce(f32[2048]{0:T(1024)S(1)} %bitcast.130), channel_id=3, replica_groups=mesh['nodes'=16,'cols'=8] {'cols'}, use_global_device_ids=true, to_apply=%region_6.7.clone | all-reduce | flops 2048 | bytes 16384
  289.6 18.8 %reduce-scatter.3.cloned.1.call-done = f32[256,256]{1,0:T(8,128)} async-done(((f32[2048,256]{1,0:T(8,128)}), f32[256,256]{1,0:T(8,128)}) %reduce-scatter.3.cloned.1.call-update) | async-done | bytes 262160 | tf_op jit(solution)/shard_map/reduce_scatter | solution.py:72
  314.1 20.1 %all-gather.2.cloned.1.call-done = bf16[2048,256]{1,0:T(8,128)(2,1)} async-done(((bf16[256,256]{1,0:T(8,128)(2,1)}), bf16[2048,256]{1,0:T(8,128)(2,1)}) %all-gather.2.cloned.1.call-update) | async-done | bytes 1048592 | tf_op jit(solution)/shard_map/all_gather | solution.py:100
  336.7 166.0 %while.23 = (s32[]{:T(128)}, f32[32,128,256]{2,1,0:T(8,128)}, s32[11,32]{1,0:T(8,128)}, s32[11,32,16,128]{3,2,1,0:T(8,128)}, s32[11,32]{1,0:T(8,128)}, /*index=5*/bf16[16,128,256]{2,1,0:T(8,128)(2,1)S(1)}, s32[]{:T(128)}) while((s32[]{:T(128)}, f32[32,128,256]{2,1,0:T(8,128)}, s32[11,32]{1,0:T(8,128)}, s32[11,32,16,128]{3,2,1,0:T(8,128)}, ...), condition=%wide.region_9.10_spmd, body=%wide.region_7.9_spmd.sunk | while | flops 271058112 | bytes 23862236 | solution.py:110
  341.9 9.9 %scatter_fusion.1 = f32[32,128,256]{2,1,0:T(8,128)} fusion(f32[32,128,256]{2,1,0:T(8,128)} %get-tuple-element.255, s32[32]{0:T(128)S(1)} %get-tuple-element.221, f32[32,128,256]{2,1,0:T(8,128)} %fusion.62), kind=kCustom, calls=%fused_computation.5.clone.1 | custom fusion | flops 1048576 | bytes 12583040 | tf_op jit(solution)/shard_map/while/body/eval_jaxpr/scatter-add | solution.py:108
  357.0 9.9 %scatter_fusion.1 = f32[32,128,256]{2,1,0:T(8,128)} fusion(f32[32,128,256]{2,1,0:T(8,128)} %get-tuple-element.255, s32[32]{0:T(128)S(1)} %get-tuple-element.221, f32[32,128,256]{2,1,0:T(8,128)} %fusion.62), kind=kCustom, calls=%fused_computation.5.clone.1 | custom fusion | flops 1048576 | bytes 12583040 | tf_op jit(solution)/shard_map/while/body/eval_jaxpr/scatter-add | solution.py:108
  372.1 9.8 %scatter_fusion.1 = f32[32,128,256]{2,1,0:T(8,128)} fusion(f32[32,128,256]{2,1,0:T(8,128)} %get-tuple-element.255, s32[32]{0:T(128)S(1)} %get-tuple-element.221, f32[32,128,256]{2,1,0:T(8,128)} %fusion.62), kind=kCustom, calls=%fused_computation.5.clone.1 | custom fusion | flops 1048576 | bytes 12583040 | tf_op jit(solution)/shard_map/while/body/eval_jaxpr/scatter-add | solution.py:108
  387.1 9.9 %scatter_fusion.1 = f32[32,128,256]{2,1,0:T(8,128)} fusion(f32[32,128,256]{2,1,0:T(8,128)} %get-tuple-element.255, s32[32]{0:T(128)S(1)} %get-tuple-element.221, f32[32,128,256]{2,1,0:T(8,128)} %fusion.62), kind=kCustom, calls=%fused_computation.5.clone.1 | custom fusion | flops 1048576 | bytes 12583040 | tf_op jit(solution)/shard_map/while/body/eval_jaxpr/scatter-add | solution.py:108
  402.2 9.9 %scatter_fusion.1 = f32[32,128,256]{2,1,0:T(8,128)} fusion(f32[32,128,256]{2,1,0:T(8,128)} %get-tuple-element.255, s32[32]{0:T(128)S(1)} %get-tuple-element.221, f32[32,128,256]{2,1,0:T(8,128)} %fusion.62), kind=kCustom, calls=%fused_computation.5.clone.1 | custom fusion | flops 1048576 | bytes 12583040 | tf_op jit(solution)/shard_map/while/body/eval_jaxpr/scatter-add | solution.py:108
  417.3 9.9 %scatter_fusion.1 = f32[32,128,256]{2,1,0:T(8,128)} fusion(f32[32,128,256]{2,1,0:T(8,128)} %get-tuple-element.255, s32[32]{0:T(128)S(1)} %get-tuple-element.221, f32[32,128,256]{2,1,0:T(8,128)} %fusion.62), kind=kCustom, calls=%fused_computation.5.clone.1 | custom fusion | flops 1048576 | bytes 12583040 | tf_op jit(solution)/shard_map/while/body/eval_jaxpr/scatter-add | solution.py:108
  432.4 10.1 %scatter_fusion.1 = f32[32,128,256]{2,1,0:T(8,128)} fusion(f32[32,128,256]{2,1,0:T(8,128)} %get-tuple-element.255, s32[32]{0:T(128)S(1)} %get-tuple-element.221, f32[32,128,256]{2,1,0:T(8,128)} %fusion.62), kind=kCustom, calls=%fused_computation.5.clone.1 | custom fusion | flops 1048576 | bytes 12583040 | tf_op jit(solution)/shard_map/while/body/eval_jaxpr/scatter-add | solution.py:108
  447.7 9.9 %scatter_fusion.1 = f32[32,128,256]{2,1,0:T(8,128)} fusion(f32[32,128,256]{2,1,0:T(8,128)} %get-tuple-element.255, s32[32]{0:T(128)S(1)} %get-tuple-element.221, f32[32,128,256]{2,1,0:T(8,128)} %fusion.62), kind=kCustom, calls=%fused_computation.5.clone.1 | custom fusion | flops 1048576 | bytes 12583040 | tf_op jit(solution)/shard_map/while/body/eval_jaxpr/scatter-add | solution.py:108
  462.8 9.9 %scatter_fusion.1 = f32[32,128,256]{2,1,0:T(8,128)} fusion(f32[32,128,256]{2,1,0:T(8,128)} %get-tuple-element.255, s32[32]{0:T(128)S(1)} %get-tuple-element.221, f32[32,128,256]{2,1,0:T(8,128)} %fusion.62), kind=kCustom, calls=%fused_computation.5.clone.1 | custom fusion | flops 1048576 | bytes 12583040 | tf_op jit(solution)/shard_map/while/body/eval_jaxpr/scatter-add | solution.py:108
  477.9 9.8 %scatter_fusion.1 = f32[32,128,256]{2,1,0:T(8,128)} fusion(f32[32,128,256]{2,1,0:T(8,128)} %get-tuple-element.255, s32[32]{0:T(128)S(1)} %get-tuple-element.221, f32[32,128,256]{2,1,0:T(8,128)} %fusion.62), kind=kCustom, calls=%fused_computation.5.clone.1 | custom fusion | flops 1048576 | bytes 12583040 | tf_op jit(solution)/shard_map/while/body/eval_jaxpr/scatter-add | solution.py:108
  492.9 9.7 %scatter_fusion.1 = f32[32,128,256]{2,1,0:T(8,128)} fusion(f32[32,128,256]{2,1,0:T(8,128)} %get-tuple-element.255, s32[32]{0:T(128)S(1)} %get-tuple-element.221, f32[32,128,256]{2,1,0:T(8,128)} %fusion.62), kind=kCustom, calls=%fused_computation.5.clone.1 | custom fusion | flops 1048576 | bytes 12583040 | tf_op jit(solution)/shard_map/while/body/eval_jaxpr/scatter-add | solution.py:108
  503.3 65.7 %psum.23 = f32[256]{0:T(256)} all-reduce(f32[256]{0:T(256)S(1)} %copy-done.8), channel_id=1, replica_groups=mesh['nodes'=16,'cols'=8] {'nodes','cols'}, use_global_device_ids=true, to_apply=%region_14.15 | all-reduce | flops 256 | bytes 2048 | tf_op jit(solution)/shard_map/psum | solution.py:94
  570.9 9.9 %reduce-scatter.5.cloned.1.call-done = f32[256,256]{1,0:T(8,128)} async-done(((f32[4096,256]{1,0:T(8,128)}), f32[256,256]{1,0:T(8,128)}) %reduce-scatter.5.cloned.1.call-update) | async-done | bytes 262160 | tf_op jit(solution)/shard_map/reduce_scatter | solution.py:116
  (242 shorter events, 118.6 us)
Async XLA Ops:
  7.2 301.2 %copy-start = (bf16[256,256]{1,0:T(8,128)(2,1)S(1)}, bf16[256,256]{1,0:T(8,128)(2,1)}, u32[]{:S(2)}) copy-start(bf16[256,256]{1,0:T(8,128)(2,1)} %param.17) | copy-start | bytes 393220
  7.2 73.7 %copy-start.3 = (bf16[256,256]{1,0:T(8,128)(2,1)S(1)}, bf16[256,256]{1,0:T(8,128)(2,1)}, u32[]{:S(2)}) copy-start(bf16[256,256]{1,0:T(8,128)(2,1)} %param.12) | copy-start | bytes 393220
  7.2 301.2 %reduce-scatter.3.cloned.1.call-start = ((), (), s32[]{:S(2)}) async-start(), calls=%async_computation.2 | async-start | bytes 2359296 | tf_op jit(solution)/shard_map/reduce_scatter | solution.py:72
  7.2 10.1 %collective-permute-start = (bf16[256,256]{1,0:T(8,128)(2,1)}, bf16[256,256]{1,0:T(8,128)(2,1)S(1)}, u32[]{:S(2)}, u32[]{:S(2)}) collective-permute-start(bf16[256,256]{1,0:T(8,128)(2,1)} %param.12), channel_id=1, source_target_pairs={{0,8},{8,16},{16,24},{24,32},{32,40},{40,48},{48,56},{56,64},{64,7... | collective-permute-start | bytes 393224 | tf_op jit(solution)/shard_map/ppermute | solution.py:21
  17.3 8.3 %collective-permute-start.1 = (bf16[256,256]{1,0:T(8,128)(2,1)S(1)}, bf16[256,256]{1,0:T(8,128)(2,1)S(1)}, u32[]{:S(2)}, u32[]{:S(2)}) collective-permute-start(bf16[256,256]{1,0:T(8,128)(2,1)S(1)} %collective-permute-done), channel_id=1, source_target_pairs={{0,8},{8,16},{16,24},{24,32},{32,40},{40,48},{48,56},{56,64},{64,7... | collective-permute-start | bytes 393224 | tf_op jit(solution)/shard_map/ppermute | solution.py:21
  17.3 8.3 %collective-permute-start.8 = (bf16[256,256]{1,0:T(8,128)(2,1)}, bf16[256,256]{1,0:T(8,128)(2,1)S(1)}, u32[]{:S(2)}, u32[]{:S(2)}) collective-permute-start(bf16[256,256]{1,0:T(8,128)(2,1)} %param.12), channel_id=1, source_target_pairs={{8,0},{16,8},{24,16},{32,24},{40,32},{48,40},{56,48},{64,56},{72,6... | collective-permute-start | bytes 393224 | tf_op jit(solution)/shard_map/ppermute | solution.py:23
  25.6 8.3 %collective-permute-start.2 = (bf16[256,256]{1,0:T(8,128)(2,1)S(1)}, bf16[256,256]{1,0:T(8,128)(2,1)S(1)}, u32[]{:S(2)}, u32[]{:S(2)}) collective-permute-start(bf16[256,256]{1,0:T(8,128)(2,1)S(1)} %collective-permute-done.1), channel_id=1, source_target_pairs={{0,8},{8,16},{16,24},{24,32},{32,40},{40,48},{48,56},{56,64},{64,7... | collective-permute-start | bytes 393224 | tf_op jit(solution)/shard_map/ppermute | solution.py:21
  25.6 8.3 %collective-permute-start.9 = (bf16[256,256]{1,0:T(8,128)(2,1)S(1)}, bf16[256,256]{1,0:T(8,128)(2,1)S(1)}, u32[]{:S(2)}, u32[]{:S(2)}) collective-permute-start(bf16[256,256]{1,0:T(8,128)(2,1)S(1)} %collective-permute-done.8), channel_id=1, source_target_pairs={{8,0},{16,8},{24,16},{32,24},{40,32},{48,40},{56,48},{64,56},{72,6... | collective-permute-start | bytes 393224 | tf_op jit(solution)/shard_map/ppermute | solution.py:23
  33.9 8.3 %collective-permute-start.3 = (bf16[256,256]{1,0:T(8,128)(2,1)S(1)}, bf16[256,256]{1,0:T(8,128)(2,1)S(1)}, u32[]{:S(2)}, u32[]{:S(2)}) collective-permute-start(bf16[256,256]{1,0:T(8,128)(2,1)S(1)} %collective-permute-done.2), channel_id=1, source_target_pairs={{0,8},{8,16},{16,24},{24,32},{32,40},{40,48},{48,56},{56,64},{64,7... | collective-permute-start | bytes 393224 | tf_op jit(solution)/shard_map/ppermute | solution.py:21
  33.9 8.3 %collective-permute-start.10 = (bf16[256,256]{1,0:T(8,128)(2,1)S(1)}, bf16[256,256]{1,0:T(8,128)(2,1)S(1)}, u32[]{:S(2)}, u32[]{:S(2)}) collective-permute-start(bf16[256,256]{1,0:T(8,128)(2,1)S(1)} %collective-permute-done.9), channel_id=1, source_target_pairs={{8,0},{16,8},{24,16},{32,24},{40,32},{48,40},{56,48},{64,56},{72,6... | collective-permute-start | bytes 393224 | tf_op jit(solution)/shard_map/ppermute | solution.py:23
  42.2 8.3 %collective-permute-start.4 = (bf16[256,256]{1,0:T(8,128)(2,1)S(1)}, bf16[256,256]{1,0:T(8,128)(2,1)S(1)}, u32[]{:S(2)}, u32[]{:S(2)}) collective-permute-start(bf16[256,256]{1,0:T(8,128)(2,1)S(1)} %collective-permute-done.3), channel_id=1, source_target_pairs={{0,8},{8,16},{16,24},{24,32},{32,40},{40,48},{48,56},{56,64},{64,7... | collective-permute-start | bytes 393224 | tf_op jit(solution)/shard_map/ppermute | solution.py:21
  42.2 8.3 %collective-permute-start.11 = (bf16[256,256]{1,0:T(8,128)(2,1)S(1)}, bf16[256,256]{1,0:T(8,128)(2,1)S(1)}, u32[]{:S(2)}, u32[]{:S(2)}) collective-permute-start(bf16[256,256]{1,0:T(8,128)(2,1)S(1)} %collective-permute-done.10), channel_id=1, source_target_pairs={{8,0},{16,8},{24,16},{32,24},{40,32},{48,40},{56,48},{64,56},{72,6... | collective-permute-start | bytes 393224 | tf_op jit(solution)/shard_map/ppermute | solution.py:23
  50.5 0.7 copy-start.5
  50.5 8.9 %collective-permute-start.5 = (bf16[256,256]{1,0:T(8,128)(2,1)S(1)}, bf16[256,256]{1,0:T(8,128)(2,1)S(1)}, u32[]{:S(2)}, u32[]{:S(2)}) collective-permute-start(bf16[256,256]{1,0:T(8,128)(2,1)S(1)} %collective-permute-done.4), channel_id=1, source_target_pairs={{0,8},{8,16},{16,24},{24,32},{32,40},{40,48},{48,56},{56,64},{64,7... | collective-permute-start | bytes 393224 | tf_op jit(solution)/shard_map/ppermute | solution.py:21
  51.1 8.3 %collective-permute-start.12 = (bf16[256,256]{1,0:T(8,128)(2,1)S(1)}, bf16[256,256]{1,0:T(8,128)(2,1)S(1)}, u32[]{:S(2)}, u32[]{:S(2)}) collective-permute-start(bf16[256,256]{1,0:T(8,128)(2,1)S(1)} %collective-permute-done.11), channel_id=1, source_target_pairs={{8,0},{16,8},{24,16},{32,24},{40,32},{48,40},{56,48},{64,56},{72,6... | collective-permute-start | bytes 393224 | tf_op jit(solution)/shard_map/ppermute | solution.py:23
  59.3 17.6 %copy-start.6 = (bf16[256,256]{1,0:T(8,128)(2,1)}, bf16[256,256]{1,0:T(8,128)(2,1)S(1)}, u32[]{:S(2)}) copy-start(bf16[256,256]{1,0:T(8,128)(2,1)S(1)} %collective-permute-done.5) | copy-start | bytes 393220
  59.3 9.4 %collective-permute-start.6 = (bf16[256,256]{1,0:T(8,128)(2,1)S(1)}, bf16[256,256]{1,0:T(8,128)(2,1)S(1)}, u32[]{:S(2)}, u32[]{:S(2)}) collective-permute-start(bf16[256,256]{1,0:T(8,128)(2,1)S(1)} %collective-permute-done.5), channel_id=1, source_target_pairs={{0,8},{8,16},{16,24},{24,32},{32,40},{40,48},{48,56},{56,64},{64,7... | collective-permute-start | bytes 393224 | tf_op jit(solution)/shard_map/ppermute | solution.py:21
  59.4 12.1 %collective-permute-start.13 = (bf16[256,256]{1,0:T(8,128)(2,1)S(1)}, bf16[256,256]{1,0:T(8,128)(2,1)}, u32[]{:S(2)}, u32[]{:S(2)}) collective-permute-start(bf16[256,256]{1,0:T(8,128)(2,1)S(1)} %collective-permute-done.12), channel_id=1, source_target_pairs={{8,0},{16,8},{24,16},{32,24},{40,32},{48,40},{56,48},{64,56},{72,6... | collective-permute-start | bytes 393224 | tf_op jit(solution)/shard_map/ppermute | solution.py:23
  68.7 8.2 %copy-start.7 = (bf16[256,256]{1,0:T(8,128)(2,1)}, bf16[256,256]{1,0:T(8,128)(2,1)S(1)}, u32[]{:S(2)}) copy-start(bf16[256,256]{1,0:T(8,128)(2,1)S(1)} %collective-permute-done.6) | copy-start | bytes 393220
  68.7 8.4 %collective-permute-start.7 = (bf16[256,256]{1,0:T(8,128)(2,1)S(1)}, bf16[256,256]{1,0:T(8,128)(2,1)}, u32[]{:S(2)}, u32[]{:S(2)}) collective-permute-start(bf16[256,256]{1,0:T(8,128)(2,1)S(1)} %collective-permute-done.6), channel_id=1, source_target_pairs={{0,8},{8,16},{16,24},{24,32},{32,40},{40,48},{48,56},{56,64},{64,7... | collective-permute-start | bytes 393224 | tf_op jit(solution)/shard_map/ppermute | solution.py:21
  71.5 10.4 %collective-permute-start.14 = (bf16[256,256]{1,0:T(8,128)(2,1)}, bf16[256,256]{1,0:T(8,128)(2,1)S(1)}, u32[]{:S(2)}, u32[]{:S(2)}) collective-permute-start(bf16[256,256]{1,0:T(8,128)(2,1)} %collective-permute-done.13), channel_id=1, source_target_pairs={{8,0},{16,8},{24,16},{32,24},{40,32},{48,40},{56,48},{64,56},{72,6... | collective-permute-start | bytes 393224 | tf_op jit(solution)/shard_map/ppermute | solution.py:23
  273.9 1.3 copy-start.1
  273.9 1.4 copy-start.12
  273.9 2.6 copy-start.4
  274.0 34.4 %copy-start.10 = (bf16[256,256]{1,0:T(8,128)(2,1)S(1)}, bf16[256,256]{1,0:T(8,128)(2,1)}, u32[]{:S(2)}) copy-start(bf16[256,256]{1,0:T(8,128)(2,1)} %param.19) | copy-start | bytes 393220
  274.0 34.4 %copy-start.11 = (f32[256]{0:T(256)S(1)}, f32[256]{0:T(256)}, u32[]{:S(2)}) copy-start(f32[256]{0:T(256)} %param.18) | copy-start | bytes 3076
  275.3 59.0 %all-gather.2.cloned.1.call-start = ((), (), s32[]{:S(2)}) async-start(), calls=%async_computation.3 | async-start | bytes 1179648 | tf_op jit(solution)/shard_map/all_gather | solution.py:100
  308.4 4.5 copy-start.9
  311.8 257.2 %all-reduce.4.cloned.1.call-start = ((), (), s32[]{:S(2)}) async-start(), calls=%async_computation.5 | async-start | bytes 1048576 | tf_op jit(solution)/shard_map/psum | solution.py:94
  313.9 266.9 %reduce-scatter.5.cloned.1.call-start = ((), (), s32[]{:S(2)}) async-start(), calls=%async_computation.4 | async-start | bytes 4456448 | tf_op jit(solution)/shard_map/reduce_scatter | solution.py:116
  334.2 2.4 copy-start.2
  502.7 0.7 copy-start.8
Sparse Core Ops, SparseCore 0:
  275.4 32.9 reduce-scatter.2
  312.0 22.2 all-gather.1
  339.8 144.6 all-reduce.3
  502.8 77.9 reduce-scatter.4
